TPU v7x, 512 devices: a whole 4x8x8 slice. The times are simulated.
512 devices in a mesh: bin: 64 (over z, y), wave: 8 (over x, core).
Axes of the slice: x: 4, y: 8, z: 8, core: 2. Of those that a mesh axis runs over, the one named last changes fastest.
Arguments:
- sources: bfloat16 [262144, 256], P(('bin', 'wave')), may hold values from -6 to 6
- density: bfloat16 [262144], P(('bin', 'wave')), may hold values from 0.5 to 1.5
- temp_bins: int32 [262144, 1], P(('bin', 'wave')), may hold values from 0 to 63; in each aligned block of 512 rows (0 to 511, 512 to 1023, ...) at most 16 rows name the same one
- ray_index: int32 [262144], P(('bin', 'wave')), may hold values from 0 to 1023
- rate_tables: bfloat16 [64, 256, 256], P('bin'), as said below
- line_table: bfloat16 [256, 8192], P(None, 'wave'), may hold values from -0.0234375 to 0.0234375
Outputs:
- intensity: float32 [1024, 8192], P('bin', 'wave')
Inputs may be any that keep to these rules, and one draw needn't show every extreme that they name: `temp_bins`: among the 512 cells of one device (aligned blocks of 512 rows) no bin is named more than 16 times; some bin is named exactly 16 times. `rate_tables`: each bin's matrix has a diagonal between 0.25 and 0.55 and independent off-diagonal entries.
All inputs are finite; a program needn't handle non-finite values.
Results may differ from a plain program's by a relative error of at most 0.005.
Values may be sent and summed in bfloat16 or wider, within the bound.
A program may use at most 64 MiB of HBM per device.

v0:
```python
import jax
import jax.numpy as jnp
from jax import lax
from jax.sharding import PartitionSpec as P

RAY_DEV = 16


def iterate_levels(src_rows, den_rows, table):
    den_col = den_rows[:, None].astype(jnp.float32)
    src_wide = src_rows.astype(jnp.float32)
    first = (
        den_col * jnp.dot(src_rows, table, preferred_element_type=jnp.float32) + src_wide
    ).astype(jnp.bfloat16)
    second = (
        den_col * jnp.dot(first, table, preferred_element_type=jnp.float32) + src_wide
    ).astype(jnp.bfloat16)
    return second


def line_product(whole_rays, line_table):
    return jnp.dot(
        whole_rays,
        line_table.astype(jnp.float32),
        precision=lax.Precision.HIGHEST,
        preferred_element_type=jnp.float32,
    )


def per_device(sources, density, temp_bins, ray_index, rate_tables, line_table):
    cell_count, level_count = sources.shape
    bin_total = lax.axis_size("bin")
    capacity = max(2, 2 * cell_count // bin_total)
    ray_total = RAY_DEV * bin_total
    bin_of = temp_bins[:, 0]
    member = (bin_of[:, None] == jnp.arange(bin_total, dtype=jnp.int32)[None, :]).astype(jnp.int32)
    position = jnp.sum(jnp.cumsum(member, axis=0) * member, axis=1) - 1
    slot_index = bin_of * capacity + position
    outgoing = (
        jnp.zeros((bin_total * capacity, level_count), sources.dtype).at[slot_index].set(sources)
    )
    outgoing = outgoing.reshape(bin_total, capacity, level_count)
    out_density = jnp.zeros((bin_total * capacity,), density.dtype).at[slot_index].set(density)
    out_density = out_density.reshape(bin_total, capacity)
    populations = None
    table = rate_tables[0]
    src_rows = lax.all_to_all(outgoing, "bin", split_axis=0, concat_axis=0, tiled=True)
    den_rows = lax.all_to_all(out_density, "bin", split_axis=0, concat_axis=0, tiled=True)
    shape_rows = src_rows.shape
    populated = iterate_levels(src_rows.reshape(-1, level_count), den_rows.reshape(-1), table)
    populated = populated.reshape(shape_rows)
    returned = lax.all_to_all(populated, "bin", split_axis=0, concat_axis=0, tiled=True)
    populations = returned.reshape(bin_total * capacity, level_count)[slot_index]
    local_sums = jax.ops.segment_sum(
        populations.astype(jnp.float32), ray_index, num_segments=ray_total
    )
    own_rays = lax.psum_scatter(local_sums, "bin", scatter_dimension=0, tiled=True)
    whole_rays = lax.psum(own_rays, "wave")
    return line_product(whole_rays, line_table)


def solution(mesh):
    in_specs = (
        P(("bin", "wave"), None),
        P(("bin", "wave")),
        P(("bin", "wave"), None),
        P(("bin", "wave")),
        P("bin", None, None),
        P(None, "wave"),
    )
    out_specs = P("bin", "wave")
    return jax.shard_map(
        per_device, mesh=mesh, in_specs=in_specs, out_specs=out_specs, check_vma=False
    )
```

profile of v0, /device:TPU:1, one launch (start us, length us, event | category | flops | bytes accessed | tf_op | source)
XLA Modules:
  0.0 368.7 jit_solution(279416597395807116)
XLA Ops:
  6.5 0.8 fusion.14
  7.3 1.2 reduce-window.6
  8.5 0.2 slice_reduce_fusion
  8.8 0.7 copy-done.1
  9.5 0.1 fusion.11
  9.6 3.9 %scatter_custom_fusion = bf16[1024]{0:T(1024)(128)(2,1)S(1)} fusion(s32[512]{0:T(512)S(1)} %bitcast.36, bf16[512]{0:T(512)(128)(2,1)} %param.7, bf16[]{:T(256)} %constant.7.clone.1), kind=kCustom, calls=%fused_computation.29 | custom fusion | bytes 2560 | tf_op jit(solution)/shard_map/scatter | solution.py:43
  13.5 0.7 all_to_all.16
  14.2 17.1 %all-to-all-start = ((bf16[64,1,16]{2,1,0:T(2,128)(2,1)}), bf16[64,1,16]{2,1,0:T(2,128)(2,1)S(1)}, u32[]{:S(2)}, u32[]{:S(2)}) async-start(bf16[64,1,16]{2,1,0:T(2,128)(2,1)} %all_to_all.16), calls=%async_computation | async-start | bytes 65536 | tf_op jit(solution)/shard_map/all_to_all | solution.py:48
  31.4 3.5 scatter_custom_fusion.1
  34.9 7.3 %all-to-all-done = bf16[64,1,16]{2,1,0:T(2,128)(2,1)S(1)} async-done(((bf16[64,1,16]{2,1,0:T(2,128)(2,1)}), bf16[64,1,16]{2,1,0:T(2,128)(2,1)S(1)}, u32[]{:S(2)}, u32[]{:S(2)}) %all-to-all-start) | async-done | bytes 2080 | tf_op jit(solution)/shard_map/all_to_all | solution.py:48
  42.2 5.0 %all-to-all-start.1 = ((bf16[64,16,256]{2,1,0:T(8,128)(2,1)}), bf16[64,16,256]{2,1,0:T(8,128)(2,1)S(1)}, u32[]{:S(2)}, u32[]{:S(2)}) async-start(bf16[64,16,256]{2,1,0:T(8,128)(2,1)} %bitcast.5), calls=%async_computation.1 | async-start | bytes 1048576 | tf_op jit(solution)/shard_map/all_to_all | solution.py:47
  47.2 0.1 convert_reduce_fusion
  47.3 0.1 reshape.56
  47.3 15.6 %all-to-all-done.1 = bf16[64,16,256]{2,1,0:T(8,128)(2,1)S(1)} async-done(((bf16[64,16,256]{2,1,0:T(8,128)(2,1)}), bf16[64,16,256]{2,1,0:T(8,128)(2,1)S(1)}, u32[]{:S(2)}, u32[]{:S(2)}) %all-to-all-start.1) | async-done | bytes 524320 | tf_op jit(solution)/shard_map/all_to_all | solution.py:47
  62.9 1.3 fusion.3
  64.3 7.7 %all-to-all-start.2 = ((bf16[64,16,256]{2,1,0:T(8,128)(2,1)}), bf16[64,16,256]{2,1,0:T(8,128)(2,1)S(1)}, u32[]{:S(2)}, u32[]{:S(2)}) async-start(bf16[64,16,256]{2,1,0:T(8,128)(2,1)} %bitcast.8), calls=%async_computation.2 | async-start | bytes 1048576 | tf_op jit(solution)/shard_map/all_to_all | solution.py:52
  72.0 0.2 reduce-scatter.2.cloned.1.call-start
  72.2 15.5 %all-to-all-done.2 = bf16[64,16,256]{2,1,0:T(8,128)(2,1)S(1)} async-done(((bf16[64,16,256]{2,1,0:T(8,128)(2,1)}), bf16[64,16,256]{2,1,0:T(8,128)(2,1)S(1)}, u32[]{:S(2)}, u32[]{:S(2)}) %all-to-all-start.2) | async-done | bytes 524320 | tf_op jit(solution)/shard_map/all_to_all | solution.py:52
  87.7 5.9 %scatter_custom_fusion.2 = f32[1024,256]{1,0:T(8,128)} fusion(s32[512]{0:T(512)} %param.9, f32[]{:T(128)} %constant.6.clone.1, bf16[1024,256]{1,0:T(8,128)(2,1)S(1)} %bitcast.32, s32[1024]{0:T(1024)S(1)} %pad_clamp_fusion), kind=kCustom, calls=%fused_computation.10 | custom fusion | flops 262144 | bytes 1577472 | tf_op jit(solution)/shard_map/scatter-add | solution.py:54
  93.6 0.0 reduce-scatter.2.cloned.1.call-update
  93.6 241.2 %reduce-scatter.2.cloned.1.call-done = f32[16,256]{1,0:T(8,128)} async-done(((f32[1024,256]{1,0:T(8,128)}), f32[16,256]{1,0:T(8,128)}) %reduce-scatter.2.cloned.1.call-update) | async-done | bytes 16400 | tf_op jit(solution)/shard_map/reduce_scatter | solution.py:57
  334.8 26.1 %psum.7 = f32[16,256]{1,0:T(8,128)S(1)} all-reduce(f32[16,256]{1,0:T(8,128)} %reduce-scatter.2.cloned.1.call-done), channel_id=1, replica_groups=mesh['bin'=64,'wave'=8] {'wave'}, use_global_device_ids=true, to_apply=%region_7.8 | all-reduce | flops 4096 | bytes 32768 | tf_op jit(solution)/shard_map/psum | solution.py:58
  360.9 0.0 copy-done
  360.9 1.0 fusion.18
  (9 shorter events, 0.1 us)
Async XLA Ops:
  6.5 354.3 %copy-start = (bf16[256,1024]{1,0:T(8,128)(2,1)S(1)}, bf16[256,1024]{1,0:T(8,128)(2,1)}, u32[]{:S(2)}) copy-start(bf16[256,1024]{1,0:T(8,128)(2,1)} %param.11) | copy-start | bytes 1572868
  8.8 0.7 copy-start.1
  14.2 27.9 %all-to-all-start = ((bf16[64,1,16]{2,1,0:T(2,128)(2,1)}), bf16[64,1,16]{2,1,0:T(2,128)(2,1)S(1)}, u32[]{:S(2)}, u32[]{:S(2)}) async-start(bf16[64,1,16]{2,1,0:T(2,128)(2,1)} %all_to_all.16), calls=%async_computation | async-start | bytes 65536 | tf_op jit(solution)/shard_map/all_to_all | solution.py:48
  42.2 20.8 %copy-start.2 = (bf16[1,256,256]{2,1,0:T(8,128)(2,1)S(1)}, bf16[1,256,256]{2,1,0:T(8,128)(2,1)}, u32[]{:S(2)}) copy-start(bf16[1,256,256]{2,1,0:T(8,128)(2,1)} %param.10) | copy-start | bytes 393220
  42.2 20.8 %all-to-all-start.1 = ((bf16[64,16,256]{2,1,0:T(8,128)(2,1)}), bf16[64,16,256]{2,1,0:T(8,128)(2,1)S(1)}, u32[]{:S(2)}, u32[]{:S(2)}) async-start(bf16[64,16,256]{2,1,0:T(8,128)(2,1)} %bitcast.5), calls=%async_computation.1 | async-start | bytes 1048576 | tf_op jit(solution)/shard_map/all_to_all | solution.py:47
  64.3 23.4 %all-to-all-start.2 = ((bf16[64,16,256]{2,1,0:T(8,128)(2,1)}), bf16[64,16,256]{2,1,0:T(8,128)(2,1)S(1)}, u32[]{:S(2)}, u32[]{:S(2)}) async-start(bf16[64,16,256]{2,1,0:T(8,128)(2,1)} %bitcast.8), calls=%async_computation.2 | async-start | bytes 1048576 | tf_op jit(solution)/shard_map/all_to_all | solution.py:52
  72.0 262.8 %reduce-scatter.2.cloned.1.call-start = ((), (), s32[]{:S(2)}) async-start(), calls=%async_computation.4 | async-start | bytes 1064960 | tf_op jit(solution)/shard_map/reduce_scatter | solution.py:57
Sparse Core Ops, SparseCore 0:
  93.7 241.0 reduce-scatter.1
where the time goes:
time: 371 us; the launch traced here: 369 us
  waiting for transfers between devices  280 us (75%)
  starting transfers between devices  30 us (8%)
  blocking collectives  26.1 us (7%)
  between operations  13.5 us (4%)
  local copies, waits for them, and re-layouts  9.15 us (2%)
  other arithmetic  8.09 us (2%)
    reduce_scatter x1, waiting for transfers between devices, per_device(): lax.psum_scatter(local_sums, 'bin', scatter_dimension=0, tiled=True)  241 us
    psum x1, blocking collectives, per_device(): whole_rays = lax.psum(own_rays, 'wave')  26.1 us
    all_to_all x1, starting transfers between devices, per_device(): lax.all_to_all(out_density, 'bin', split_axis=0, concat_axis=0, tiled=True)  17.1 us
    all_to_all x1, waiting for transfers between devices, per_device(): lax.all_to_all(outgoing, 'bin', split_axis=0, concat_axis=0, tiled=True)  15.6 us
    all_to_all x1, waiting for transfers between devices, per_device(): lax.all_to_all(populated, 'bin', split_axis=0, concat_axis=0, tiled=True)  15.5 us
    all_to_all x1, starting transfers between devices, per_device(): lax.all_to_all(populated, 'bin', split_axis=0, concat_axis=0, tiled=True)  7.67 us
  transfers between devices with their start and end apart: 4, of which 4 were waited for; matrix products, arithmetic and copies ran while one was open for 1% of the time, Pallas kernels for 0%

commit v1 on v0

v1 whole, which is shorter than its diff:
```python
import jax
import jax.numpy as jnp
from jax import lax
from jax.experimental import pallas as pl
from jax.experimental.pallas import tpu as pltpu
from jax.sharding import PartitionSpec as P

MESH = pl.DeviceIdType.MESH
F32 = jnp.float32
BF16 = jnp.bfloat16
N_BIN = 64
N_WAVE = 8
SIDE = 8
CAP = 16
CELLS = 512
LEVELS = 256
RAYS = 1024
CHUNKS = 4
PER = N_BIN // CHUNKS
ROWS = PER * CAP


def iota(shape, dim):
    return lax.broadcasted_iota(jnp.int32, shape, dim)


def nt(a, b):
    return lax.dot_general(a, b, (((1,), (1,)), ((), ())), preferred_element_type=F32)


def mm(a, b):
    return jnp.dot(a, b, preferred_element_type=F32)


def as_row(ref):
    v = ref[...]
    return jnp.concatenate([v[i : i + 1, :] for i in range(v.shape[0])], axis=1)


def kernel(
    src_ref, den_ref, bins_ref, ray_ref, tab_ref, out_ref,
    send, esend, recv, erecv, acc, sbuf, crecv, xsend, xrecv, ysend, yrecv, asend, arecv,
    s_sem, e_ssem, r_sem, e_rsem, c_ssem, c_rsem, x_ssem, x_rsem, y_ssem, y_rsem, a_ssem, a_rsem,
):
    me = lax.axis_index("bin")
    wave = lax.axis_index("wave")
    mz, my = me // SIDE, lax.rem(me, SIDE)
    mx, core = wave // 2, lax.rem(wave, 2)

    def peer(i):
        tz = lax.rem(mz + i // SIDE, SIDE)
        ty = lax.rem(my + lax.rem(i, SIDE), SIDE)
        return tz * SIDE + ty

    barrier = pltpu.get_barrier_semaphore()

    @pl.loop(1, N_BIN)
    def _(i):
        pl.semaphore_signal(barrier, inc=1, device_id=(peer(i), wave), device_id_type=MESH)

    @pl.loop(1, N_WAVE)
    def _(i):
        pl.semaphore_signal(
            barrier, inc=1, device_id=(me, lax.rem(wave + i, N_WAVE)), device_id_type=MESH
        )

    bins = as_row(bins_ref)
    den = as_row(den_ref)
    ray = as_row(ray_ref)
    code = ((ray & 15) >> 1) * (2 * N_BIN) + (ray >> 4) * 2 + (ray & 1)
    high = (code >> 5).astype(F32)
    low = (code & 31).astype(F32)
    member = jnp.where(iota((N_BIN, CELLS), 0) == bins, 1.0, 0.0)
    upper = jnp.where(iota((CELLS, CELLS), 0) <= iota((CELLS, CELLS), 1), 1.0, 0.0).astype(BF16)
    rank = mm(member.astype(BF16), upper)
    pos = (jnp.sum(rank * member, axis=0, keepdims=True) - 1.0).astype(jnp.int32)
    slot = bins * CAP + pos
    lane = iota((128, CELLS), 0)
    extras = jnp.zeros((N_BIN, 128), F32)
    for k, value in enumerate((den, high, low)):
        place = jnp.where(lane == pos + k * CAP, 1.0, 0.0).astype(BF16)
        extras = extras + nt((member * value).astype(BF16), place)
    for b in range(N_BIN):
        esend[b] = extras[b : b + 1, :]

    @pl.loop(0, CHUNKS)
    def _(c):
        hot = jnp.where(iota((ROWS, CELLS), 0) + c * ROWS == slot, 1.0, 0.0).astype(BF16)
        packed = mm(hot, src_ref[...]).astype(BF16)
        send[pl.ds(c * PER, PER)] = packed.reshape(PER, CAP, LEVELS)

    acc[...] = jnp.zeros_like(acc)
    pl.semaphore_wait(barrier, N_BIN + N_WAVE - 2)

    @pl.loop(1, N_BIN)
    def _(i):
        to = peer(i)
        pltpu.make_async_remote_copy(
            src_ref=esend.at[to], dst_ref=erecv.at[me], send_sem=e_ssem, recv_sem=e_rsem,
            device_id=(to, wave), device_id_type=MESH,
        ).start()
        pltpu.make_async_remote_copy(
            src_ref=send.at[to], dst_ref=recv.at[me], send_sem=s_sem, recv_sem=r_sem.at[me // PER],
            device_id=(to, wave), device_id_type=MESH,
        ).start()

    pltpu.make_async_copy(esend.at[me], erecv.at[me], e_rsem).start()
    pltpu.make_async_copy(send.at[me], recv.at[me], r_sem.at[me // PER]).start()
    pltpu.make_async_copy(erecv, erecv, e_rsem).wait()

    ones = jnp.ones((128, LEVELS), BF16)
    ones8 = jnp.ones((8, 128), BF16)

    @pl.loop(0, CHUNKS)
    def _(k):
        c = lax.rem(me // PER + k, CHUNKS)
        block = pl.ds(c * PER, PER)
        pltpu.make_async_copy(recv.at[block], recv.at[block], r_sem.at[c]).wait()
        extra = jnp.broadcast_to(erecv[block], (PER, CAP, 128)).reshape(ROWS, 128)
        lanes = iota((ROWS, 128), 1)
        own = iota((ROWS, 128), 0) & (CAP - 1)
        dens = mm(jnp.where(lanes == own, extra, 0.0).astype(BF16), ones)
        coded = jnp.where(
            lanes == own + CAP, extra * 32.0, jnp.where(lanes == own + 2 * CAP, extra, 0.0)
        )
        rays = nt(ones8, coded.astype(BF16))[0:1, :].astype(jnp.int32)
        rows = recv[block].reshape(ROWS, LEVELS)
        wide = rows.astype(F32)
        table = tab_ref[...]
        first = (dens * mm(rows, table) + wide).astype(BF16)
        pops = (dens * mm(first, table) + wide).astype(BF16)
        hot = jnp.where(iota((RAYS, ROWS), 0) == rays, 1.0, 0.0).astype(BF16)
        acc[...] += mm(hot, pops)

    block_rows = RAYS // N_WAVE
    sibling = mx * 2 + 1 - core

    def pair_copy(i):
        tx = lax.rem(mx + i, 4)
        return tx, pltpu.make_async_remote_copy(
            src_ref=sbuf.at[tx], dst_ref=crecv.at[tx], send_sem=c_ssem.at[tx],
            recv_sem=c_rsem.at[tx], device_id=(me, sibling), device_id_type=MESH,
        )

    def x_copy(i):
        tx = lax.rem(mx + i, 4)
        return pltpu.make_async_remote_copy(
            src_ref=xsend.at[tx], dst_ref=xrecv.at[i - 1], send_sem=x_ssem.at[i - 1],
            recv_sem=x_rsem.at[i - 1], device_id=(me, tx * 2 + core), device_id_type=MESH,
        )

    for i in (2, 1, 3, 0):
        tx, copy = pair_copy(i)
        start = pl.multiple_of((tx * 2 + 1 - core) * block_rows, block_rows)
        sbuf[tx] = acc[pl.ds(start, block_rows), :].astype(BF16)
        copy.start()
    total = None
    for i in (2, 1, 3, 0):
        tx, copy = pair_copy(i)
        copy.wait_recv()
        start = pl.multiple_of((tx * 2 + core) * block_rows, block_rows)
        total = acc[pl.ds(start, block_rows), :] + crecv[tx].astype(F32)
        if i != 0:
            xsend[tx] = total.astype(BF16)
            x_copy(i).start()
    for i in (1, 3, 2):
        x_copy(i).wait_recv()
        total = total + xrecv[i - 1].astype(F32)

    for b in range(N_BIN):
        ysend[b] = total[2 * b : 2 * b + 2, :]

    @pl.loop(1, N_BIN)
    def _(i):
        to = peer(i)
        pltpu.make_async_remote_copy(
            src_ref=ysend.at[to], dst_ref=yrecv.at[me], send_sem=y_ssem, recv_sem=y_rsem,
            device_id=(to, wave), device_id_type=MESH,
        ).start()

    pltpu.make_async_copy(ysend.at[me], yrecv.at[me], y_rsem).start()
    pltpu.make_async_copy(yrecv, yrecv, y_rsem).wait()
    asend[...] = jnp.sum(yrecv[...], axis=0)

    @pl.loop(1, N_WAVE)
    def _(i):
        pltpu.make_async_remote_copy(
            src_ref=asend, dst_ref=arecv.at[wave], send_sem=a_ssem, recv_sem=a_rsem,
            device_id=(me, lax.rem(wave + i, N_WAVE)), device_id_type=MESH,
        ).start()

    pltpu.make_async_copy(asend, arecv.at[wave], a_rsem).start()
    pltpu.make_async_copy(arecv, arecv, a_rsem).wait()
    for w in range(N_WAVE):
        out_ref[2 * w : 2 * w + 2, :] = arecv[w]

    rest = pl.ds(0, N_BIN - 1)
    pltpu.make_async_copy(esend.at[rest], esend.at[rest], e_ssem).wait()
    pltpu.make_async_copy(send.at[rest], send.at[rest], s_sem).wait()
    for i in (2, 1, 3, 0):
        pair_copy(i)[1].wait_send()
    for i in (1, 2, 3):
        x_copy(i).wait_send()
    pltpu.make_async_copy(ysend.at[rest], ysend.at[rest], y_ssem).wait()
    others = pl.ds(0, N_WAVE - 1)
    pltpu.make_async_copy(arecv.at[others], arecv.at[others], a_ssem).wait()


def per_device(sources, density, temp_bins, ray_index, rate_tables, line_table):
    vmem = pl.BlockSpec(memory_space=pltpu.VMEM)
    dma = pltpu.SemaphoreType.DMA
    block = RAYS // N_WAVE
    whole_rays = pl.pallas_call(
        kernel,
        out_shape=jax.ShapeDtypeStruct((RAYS // N_BIN, LEVELS), F32),
        in_specs=[vmem] * 5,
        out_specs=vmem,
        scratch_shapes=[
            pltpu.VMEM((N_BIN, CAP, LEVELS), BF16),
            pltpu.VMEM((N_BIN, 1, 128), F32),
            pltpu.VMEM((N_BIN, CAP, LEVELS), BF16),
            pltpu.VMEM((N_BIN, 1, 128), F32),
            pltpu.VMEM((RAYS, LEVELS), F32),
            pltpu.VMEM((4, block, LEVELS), BF16),
            pltpu.VMEM((4, block, LEVELS), BF16),
            pltpu.VMEM((4, block, LEVELS), BF16),
            pltpu.VMEM((3, block, LEVELS), BF16),
            pltpu.VMEM((N_BIN, 2, LEVELS), F32),
            pltpu.VMEM((N_BIN, 2, LEVELS), F32),
            pltpu.VMEM((2, LEVELS), F32),
            pltpu.VMEM((N_WAVE, 2, LEVELS), F32),
            dma, dma, dma((CHUNKS,)), dma, dma((4,)), dma((4,)), dma((3,)), dma((3,)),
            dma, dma, dma, dma,
        ],
        compiler_params=pltpu.CompilerParams(collective_id=0, has_side_effects=True),
        name="populations",
    )(
        sources,
        density.astype(F32).reshape(4, 128),
        temp_bins.reshape(4, 128),
        ray_index.reshape(4, 128),
        rate_tables[0],
    )
    return jnp.dot(
        whole_rays,
        line_table.astype(F32),
        precision=lax.Precision.HIGHEST,
        preferred_element_type=F32,
    )


def solution(mesh):
    in_specs = (
        P(("bin", "wave"), None),
        P(("bin", "wave")),
        P(("bin", "wave"), None),
        P(("bin", "wave")),
        P("bin", None, None),
        P(None, "wave"),
    )
    return jax.shard_map(
        per_device, mesh=mesh, in_specs=in_specs, out_specs=P("bin", "wave"), check_vma=False
    )
```

time: 371 us -> 62.9 us (0.17)
  waiting for transfers between devices: 280 us -> 0 us
  Pallas kernels: 0 us -> 59.7 us
  starting transfers between devices: 30 us -> 0 us
  blocking collectives: 26.1 us -> 0 us
  between operations: 13.5 us -> 0.02 us
  local copies, waits for them, and re-layouts: 9.15 us -> 0.74 us
  other arithmetic: 8.09 us -> 0.58 us
    reduce_scatter x1 -> x0, waiting for transfers between devices: 241 us -> none  [per_device(): lax.psum_scatter(local_sums, 'bin', scatter_dimension=0, tiled=True)]
    pallas_call x0 -> x1, Pallas kernels: none -> 59.7 us  [per_device(): pl.pallas_call(kernel, out_shape=jax.ShapeDtypeStruct((RAYS // N_BIN, LEV...]
    all_to_all x3 -> x0, waiting for transfers between devices: 38.4 us -> none  [the longest x1 15.6 us: per_device(): lax.all_to_all(outgoing, 'bin', split_axis=0, concat_axis=0, tiled=True)]
    all_to_all x3 -> x0, starting transfers between devices: 29.8 us -> none  [the longest x1 17.1 us: per_device(): lax.all_to_all(out_density, 'bin', split_axis=0, concat_axis=0, tiled=True)]
    psum x1 -> x0, blocking collectives: 26.1 us -> none  [per_device(): whole_rays = lax.psum(own_rays, 'wave')]
    scatter x2 -> x0, local copies, waits for them, and re-layouts: 7.45 us -> none  [the longest x1 3.92 us: per_device(): jnp.zeros((bin_total * capacity,), density.dtype).at[slot_index]]
    scatter-add x1 -> x0, other arithmetic: 5.88 us -> none  [per_device(): jax.ops.segment_sum(populations.astype(jnp.float32), ray_index, num_segme...]
  transfers between devices with their start and end apart: 4 -> 0, of which waited for: 4 -> 0; matrix products, arithmetic and copies ran while one was open for 1% -> 0% of each run, Pallas kernels for 0% -> 0%
where the time goes in v1:
time: 62.9 us; the launch traced here: 62.7 us
  Pallas kernels  59.7 us (95%)
  matrix products  1.67 us (3%)
  local copies, waits for them, and re-layouts  0.74 us (1%)
    pallas_call x1, Pallas kernels, per_device(): pl.pallas_call(kernel, out_shape=jax.ShapeDtypeStruct((RAYS // N_BIN, LEV...  59.7 us
    dot_general x1, matrix products, per_device(): jnp.dot(whole_rays, line_table.astype(F32), precision=lax.Precision.HIGHE...  1.67 us

profile of v1, /device:TPU:1, one launch (start us, length us, event | category | flops | bytes accessed | tf_op | source)
XLA Modules:
  0.0 62.7 jit_solution(5220404386703585725)
XLA Ops:
  0.0 0.0 copy-start
  0.0 0.0 copy-start.1
  0.0 0.7 %copy-done.1 = bf16[512]{0:T(512)(128)(2,1)S(1)} copy-done((bf16[512]{0:T(512)(128)(2,1)S(1)}, bf16[512]{0:T(512)(128)(2,1)}, u32[]{:S(2)}) %copy-start.1) | copy-done | bytes 1048
  0.7 0.6 bitcast_convert_fusion.den_ref
  1.3 59.7 %populations.1 = f32[16,256]{1,0:T(8,128)} custom-call(bf16[512,256]{1,0:T(8,128)(2,1)} %src_ref.1, f32[4,128]{1,0:T(4,128)} %bitcast_convert_fusion.den_ref, s32[4,128]{1,0:T(4,128)} %bitcast.9, s32[4,128]{1,0:T(4,128)} %bitcast.10, bf16[256,256]{1,0:T(8,128)(2,1)} %bitcast.8), custom_call_target="tpu_custom_call" | custom-call | tf_op jit(solution)/shard_map/populations/pallas_call | solution.py:213
  61.0 0.0 copy-done
  61.0 1.7 %fusion = f32[16,1024]{1,0:T(8,128)} fusion(f32[16,256]{1,0:T(8,128)} %populations.1, bf16[256,1024]{1,0:T(8,128)(2,1)S(1)} %copy-done), kind=kOutput, calls=%fused_computation.1 | convolution fusion | flops 50331648 | bytes 606208 | tf_op jit(solution)/shard_map/dot_general | solution.py:244
Async XLA Ops:
  0.0 61.0 %copy-start = (bf16[256,1024]{1,0:T(8,128)(2,1)S(1)}, bf16[256,1024]{1,0:T(8,128)(2,1)}, u32[]{:S(2)}) copy-start(bf16[256,1024]{1,0:T(8,128)(2,1)} %param.11) | copy-start | bytes 1572868
  0.0 0.7 %copy-start.1 = (bf16[512]{0:T(512)(128)(2,1)S(1)}, bf16[512]{0:T(512)(128)(2,1)}, u32[]{:S(2)}) copy-start(bf16[512]{0:T(512)(128)(2,1)} %param.7) | copy-start | bytes 3076

commit v2 on v1

--- a/solution.py
+++ b/solution.py
@@ -20,6 +20,28 @@
 ROWS = PER * CAP
 
 
+def turned(offset):
+    return offset[1], (-offset[0]) % SIDE
+
+
+def reach(offset):
+    return sum(min(d, SIDE - d) for d in offset)
+
+
+def far_first():
+    order = []
+    offsets = [(dz, dy) for dz in range(SIDE) for dy in range(SIDE)][1:]
+    for offset in sorted(offsets, key=lambda o: (-reach(o), o)):
+        for _ in range(4):
+            if offset not in order:
+                order.append(offset)
+            offset = turned(offset)
+    return order
+
+
+ORDER = far_first()
+
+
 def iota(shape, dim):
     return lax.broadcasted_iota(jnp.int32, shape, dim)
 
@@ -32,14 +54,15 @@
     return jnp.dot(a, b, preferred_element_type=F32)
 
 
-def as_row(ref):
-    v = ref[...]
+def as_row(ref, dtype=jnp.int32):
+    v = ref[...].astype(dtype)
     return jnp.concatenate([v[i : i + 1, :] for i in range(v.shape[0])], axis=1)
 
 
 def kernel(
-    src_ref, den_ref, bins_ref, ray_ref, tab_ref, out_ref,
-    send, esend, recv, erecv, acc, sbuf, crecv, xsend, xrecv, ysend, yrecv, asend, arecv,
+    src_hbm, den_ref, bins_ref, ray_ref, tab_hbm, out_ref,
+    src_ref, tab_ref, load_sem,
+       send, esend, recv, erecv, acc, sbuf, crecv, xsend, xrecv, ysend, yrecv, asend, arecv,
     s_sem, e_ssem, r_sem, e_rsem, c_ssem, c_rsem, x_ssem, x_rsem, y_ssem, y_rsem, a_ssem, a_rsem,
 ):
     me = lax.axis_index("bin")
@@ -47,25 +70,24 @@
     mz, my = me // SIDE, lax.rem(me, SIDE)
     mx, core = wave // 2, lax.rem(wave, 2)
 
-    def peer(i):
-        tz = lax.rem(mz + i // SIDE, SIDE)
-        ty = lax.rem(my + lax.rem(i, SIDE), SIDE)
-        return tz * SIDE + ty
+    def peer(offset):
+        return ((mz + offset[0]) & (SIDE - 1)) * SIDE + ((my + offset[1]) & (SIDE - 1))
 
     barrier = pltpu.get_barrier_semaphore()
 
-    @pl.loop(1, N_BIN)
-    def _(i):
-        pl.semaphore_signal(barrier, inc=1, device_id=(peer(i), wave), device_id_type=MESH)
-
-    @pl.loop(1, N_WAVE)
-    def _(i):
+    for offset in ORDER:
+        pl.semaphore_signal(barrier, inc=1, device_id=(peer(offset), wave), device_id_type=MESH)
+    for i in range(1, N_WAVE):
         pl.semaphore_signal(
-            barrier, inc=1, device_id=(me, lax.rem(wave + i, N_WAVE)), device_id_type=MESH
-        )
+            barrier, inc=1, device_id=(me, (wave + i) & (N_WAVE - 1)), device_id_type=MESH
+        )
+    load_src = pltpu.make_async_copy(src_hbm, src_ref, load_sem.at[0])
+    load_tab = pltpu.make_async_copy(tab_hbm.at[0], tab_ref, load_sem.at[1])
+    load_src.start()
+    load_tab.start()
 
     bins = as_row(bins_ref)
-    den = as_row(den_ref)
+    den = as_row(den_ref, F32)
     ray = as_row(ray_ref)
     code = ((ray & 15) >> 1) * (2 * N_BIN) + (ray >> 4) * 2 + (ray & 1)
     high = (code >> 5).astype(F32)
@@ -83,6 +105,8 @@
     for b in range(N_BIN):
         esend[b] = extras[b : b + 1, :]
 
+    load_src.wait()
+
     @pl.loop(0, CHUNKS)
     def _(c):
         hot = jnp.where(iota((ROWS, CELLS), 0) + c * ROWS == slot, 1.0, 0.0).astype(BF16)
@@ -92,9 +116,8 @@
     acc[...] = jnp.zeros_like(acc)
     pl.semaphore_wait(barrier, N_BIN + N_WAVE - 2)
 
-    @pl.loop(1, N_BIN)
-    def _(i):
-        to = peer(i)
+    for offset in ORDER:
+        to = peer(offset)
         pltpu.make_async_remote_copy(
             src_ref=esend.at[to], dst_ref=erecv.at[me], send_sem=e_ssem, recv_sem=e_rsem,
             device_id=(to, wave), device_id_type=MESH,
@@ -106,6 +129,7 @@
 
     pltpu.make_async_copy(esend.at[me], erecv.at[me], e_rsem).start()
     pltpu.make_async_copy(send.at[me], recv.at[me], r_sem.at[me // PER]).start()
+    load_tab.wait()
     pltpu.make_async_copy(erecv, erecv, e_rsem).wait()
 
     ones = jnp.ones((128, LEVELS), BF16)
@@ -167,12 +191,12 @@
         x_copy(i).wait_recv()
         total = total + xrecv[i - 1].astype(F32)
 
+    total = total.astype(BF16)
     for b in range(N_BIN):
         ysend[b] = total[2 * b : 2 * b + 2, :]
 
-    @pl.loop(1, N_BIN)
-    def _(i):
-        to = peer(i)
+    for offset in ORDER:
+        to = peer(offset)
         pltpu.make_async_remote_copy(
             src_ref=ysend.at[to], dst_ref=yrecv.at[me], send_sem=y_ssem, recv_sem=y_rsem,
             device_id=(to, wave), device_id_type=MESH,
@@ -180,7 +204,7 @@
 
     pltpu.make_async_copy(ysend.at[me], yrecv.at[me], y_rsem).start()
     pltpu.make_async_copy(yrecv, yrecv, y_rsem).wait()
-    asend[...] = jnp.sum(yrecv[...], axis=0)
+    asend[...] = jnp.sum(yrecv[...].astype(F32), axis=0)
 
     @pl.loop(1, N_WAVE)
     def _(i):
@@ -208,14 +232,18 @@
 
 def per_device(sources, density, temp_bins, ray_index, rate_tables, line_table):
     vmem = pl.BlockSpec(memory_space=pltpu.VMEM)
+    hbm = pl.BlockSpec(memory_space=pl.ANY)
     dma = pltpu.SemaphoreType.DMA
     block = RAYS // N_WAVE
     whole_rays = pl.pallas_call(
         kernel,
         out_shape=jax.ShapeDtypeStruct((RAYS // N_BIN, LEVELS), F32),
-        in_specs=[vmem] * 5,
+        in_specs=[hbm, vmem, vmem, vmem, hbm],
         out_specs=vmem,
         scratch_shapes=[
+            pltpu.VMEM((CELLS, LEVELS), BF16),
+            pltpu.VMEM((LEVELS, LEVELS), BF16),
+            dma((2,)),
             pltpu.VMEM((N_BIN, CAP, LEVELS), BF16),
             pltpu.VMEM((N_BIN, 1, 128), F32),
             pltpu.VMEM((N_BIN, CAP, LEVELS), BF16),
@@ -225,8 +253,8 @@
             pltpu.VMEM((4, block, LEVELS), BF16),
             pltpu.VMEM((4, block, LEVELS), BF16),
             pltpu.VMEM((3, block, LEVELS), BF16),
-            pltpu.VMEM((N_BIN, 2, LEVELS), F32),
-            pltpu.VMEM((N_BIN, 2, LEVELS), F32),
+            pltpu.VMEM((N_BIN, 2, LEVELS), BF16),
+            pltpu.VMEM((N_BIN, 2, LEVELS), BF16),
             pltpu.VMEM((2, LEVELS), F32),
             pltpu.VMEM((N_WAVE, 2, LEVELS), F32),
             dma, dma, dma((CHUNKS,)), dma, dma((4,)), dma((4,)), dma((3,)), dma((3,)),
@@ -236,10 +264,10 @@
         name="populations",
     )(
         sources,
-        density.astype(F32).reshape(4, 128),
+        density.reshape(4, 128),
         temp_bins.reshape(4, 128),
         ray_index.reshape(4, 128),
-        rate_tables[0],
+        rate_tables,
     )
     return jnp.dot(
         whole_rays,

time: 62.9 us -> 54.1 us (0.86)
  Pallas kernels: 59.7 us -> 52.2 us
  local copies, waits for them, and re-layouts: 0.74 us -> 0.01 us
    pallas_call x1, Pallas kernels: 59.7 us -> 52.2 us  [per_device(): pl.pallas_call(kernel, out_shape=jax.ShapeDtypeStruct((RAYS // N_BIN, LEV...]
    unnamed x4 -> x2, local copies, waits for them, and re-layouts: 0.74 us -> 0.01 us
where the time goes in v2:
time: 54.1 us; the launch traced here: 53.8 us
  Pallas kernels  52.2 us (96%)
  matrix products  1.67 us (3%)
    pallas_call x1, Pallas kernels, per_device(): pl.pallas_call(kernel, out_shape=jax.ShapeDtypeStruct((RAYS // N_BIN, LEV...  52.2 us
    dot_general x1, matrix products, per_device(): jnp.dot(whole_rays, line_table.astype(F32), precision=lax.Precision.HIGHE...  1.67 us

profile of v2, /device:TPU:1, one launch (start us, length us, event | category | flops | bytes accessed | tf_op | source)
XLA Modules:
  0.0 53.8 jit_solution(362059379627226592)
XLA Ops:
  0.0 0.0 copy-start
  0.0 52.2 %populations.1 = f32[16,256]{1,0:T(8,128)} custom-call(bf16[512,256]{1,0:T(8,128)(2,1)} %src_hbm.1, bf16[4,128]{1,0:T(4,128)(2,1)} %bitcast.7, s32[4,128]{1,0:T(4,128)} %bitcast.5, s32[4,128]{1,0:T(4,128)} %bitcast.6, bf16[1,256,256]{2,1,0:T(8,128)(2,1)} %tab_hbm.1), custom_call_target="tpu_custom_call" | custom-call | tf_op jit(solution)/shard_map/populations/pallas_call | solution.py:238
  52.2 0.0 copy-done
  52.2 1.7 %fusion = f32[16,1024]{1,0:T(8,128)} fusion(f32[16,256]{1,0:T(8,128)} %populations.1, bf16[256,1024]{1,0:T(8,128)(2,1)S(1)} %copy-done), kind=kOutput, calls=%fused_computation | convolution fusion | flops 50331648 | bytes 606208 | tf_op jit(solution)/shard_map/dot_general | solution.py:272
Async XLA Ops:
  0.0 52.2 %copy-start = (bf16[256,1024]{1,0:T(8,128)(2,1)S(1)}, bf16[256,1024]{1,0:T(8,128)(2,1)}, u32[]{:S(2)}) copy-start(bf16[256,1024]{1,0:T(8,128)(2,1)} %param.11) | copy-start | bytes 1572868

commit v3 on v2

v3 whole, which is shorter than its diff:
```python
import jax
import jax.numpy as jnp
from jax import lax
from jax.experimental import pallas as pl
from jax.experimental.pallas import tpu as pltpu
from jax.sharding import PartitionSpec as P

MESH = pl.DeviceIdType.MESH
F32 = jnp.float32
BF16 = jnp.bfloat16
N_BIN = 64
N_WAVE = 8
N_X = 4
SIDE = 8
CAP = 16
CELLS = 512
LEVELS = 256
RAYS = 1024
CHUNKS = 4
PER = N_BIN // CHUNKS
ROWS = PER * CAP
PIECES = 4
PIECE_BINS = N_BIN // PIECES
PIECE = RAYS // PIECES
SHARE = PIECE // N_WAVE


def turned(offset):
    return offset[1], (-offset[0]) % SIDE


def reach(offset):
    return sum(min(d, SIDE - d) for d in offset)


def far_first():
    order = []
    offsets = [(dz, dy) for dz in range(SIDE) for dy in range(SIDE)]
    for offset in sorted(offsets, key=lambda o: (-reach(o), o)):
        for _ in range(4):
            if offset not in order:
                order.append(offset)
            offset = turned(offset)
    return order


ORDER = far_first()


def iota(shape, dim):
    return lax.broadcasted_iota(jnp.int32, shape, dim)


def nt(a, b):
    return lax.dot_general(a, b, (((1,), (1,)), ((), ())), preferred_element_type=F32)


def mm(a, b):
    return jnp.dot(a, b, preferred_element_type=F32)


def as_row(ref, dtype=jnp.int32):
    v = ref[...].astype(dtype)
    return jnp.concatenate([v[i : i + 1, :] for i in range(v.shape[0])], axis=1)


def kernel(
    src_hbm, den_hbm, bins_hbm, ray_hbm, tab_hbm, out_any,
    src_ref, den_ref, bins_ref, ray_ref, tab_ref, out_ref, load_sem,
    send, esend, recv, erecv, acc, sbuf, crecv, xsend, xrecv, ysend, yrecv, asend, arecv,
    s_sem, e_ssem, r_sem, e_rsem, c_ssem, c_rsem, x_ssem, x_rsem, y_ssem, y_rsem, a_ssem, a_rsem,
):
    me = lax.axis_index("bin")
    wave = lax.axis_index("wave")
    mz, my = me // SIDE, me & (SIDE - 1)
    mx, core = wave // 2, wave & 1

    def peer(offset):
        return ((mz + offset[0]) & (SIDE - 1)) * SIDE + ((my + offset[1]) & (SIDE - 1))

    loads = [
        pltpu.make_async_copy(given, held, load_sem.at[n])
        for n, (given, held) in enumerate((
            (bins_hbm, bins_ref), (den_hbm, den_ref), (ray_hbm, ray_ref), (src_hbm, src_ref),
            (tab_hbm.at[0], tab_ref),
        ))
    ]
    for load in loads:
        load.start()
    barrier = pltpu.get_barrier_semaphore()
    for offset in ORDER[:-1]:
        pl.semaphore_signal(barrier, inc=1, device_id=(peer(offset), wave), device_id_type=MESH)
    for i in range(1, N_WAVE):
        pl.semaphore_signal(
            barrier, inc=1, device_id=(me, (wave + i) & (N_WAVE - 1)), device_id_type=MESH
        )

    for load in loads[:3]:
        load.wait()
    bins = as_row(bins_ref)
    den = as_row(den_ref, F32)
    ray = as_row(ray_ref)
    code = (ray >> 8) * PIECE + ((ray & 15) >> 1) * SHARE + ((ray >> 4) & 15) * 2 + (ray & 1)
    high = (code >> 5).astype(F32)
    low = (code & 31).astype(F32)
    member = jnp.where(iota((N_BIN, CELLS), 0) == bins, 1.0, 0.0)
    upper = jnp.where(iota((CELLS, CELLS), 0) <= iota((CELLS, CELLS), 1), 1.0, 0.0).astype(BF16)
    rank = mm(member.astype(BF16), upper)
    pos = (jnp.sum(rank * member, axis=0, keepdims=True) - 1.0).astype(jnp.int32)
    slot = bins * CAP + pos
    lane = iota((128, CELLS), 0)
    extras = jnp.zeros((N_BIN, 128), F32)
    for k, value in enumerate((den, high, low)):
        place = jnp.where(lane == pos + k * CAP, 1.0, 0.0).astype(BF16)
        extras = extras + nt((member * value).astype(BF16), place)
    for b in range(N_BIN):
        esend[b] = extras[b : b + 1, :]
    loads[3].wait()

    @pl.loop(0, CHUNKS)
    def _(c):
        hot = jnp.where(iota((ROWS, CELLS), 0) + c * ROWS == slot, 1.0, 0.0).astype(BF16)
        packed = mm(hot, src_ref[...]).astype(BF16)
        send[pl.ds(c * PER, PER)] = packed.reshape(PER, CAP, LEVELS)

    pl.semaphore_wait(barrier, N_BIN + N_WAVE - 2)

    for k, offset in enumerate(ORDER[:-1]):
        to = peer(offset)
        for out, into, s, r in ((esend, erecv, e_ssem, e_rsem), (send, recv, s_sem, r_sem)):
            pltpu.make_async_remote_copy(
                src_ref=out.at[to], dst_ref=into.at[k], send_sem=s, recv_sem=r.at[k // PER],
                device_id=(to, wave), device_id_type=MESH,
            ).start()
    pltpu.make_async_copy(esend.at[me], erecv.at[N_BIN - 1], e_rsem.at[CHUNKS - 1]).start()
    pltpu.make_async_copy(send.at[me], recv.at[N_BIN - 1], r_sem.at[CHUNKS - 1]).start()

    acc[...] = jnp.zeros_like(acc)
    loads[4].wait()
    ones = jnp.ones((128, LEVELS), BF16)
    ones8 = jnp.ones((8, 128), BF16)

    def chunk(c):
        block = pl.ds(c * PER, PER)
        pltpu.make_async_copy(erecv.at[block], erecv.at[block], e_rsem.at[c]).wait()
        pltpu.make_async_copy(recv.at[block], recv.at[block], r_sem.at[c]).wait()
        extra = jnp.broadcast_to(erecv[block], (PER, CAP, 128)).reshape(ROWS, 128)
        lanes = iota((ROWS, 128), 1)
        own = iota((ROWS, 128), 0) & (CAP - 1)
        dens = mm(jnp.where(lanes == own, extra, 0.0).astype(BF16), ones)
        coded = jnp.where(
            lanes == own + CAP, extra * 32.0, jnp.where(lanes == own + 2 * CAP, extra, 0.0)
        )
        rays = nt(ones8, coded.astype(BF16))[0:1, :].astype(jnp.int32)
        rows = recv[block].reshape(ROWS, LEVELS)
        wide = rows.astype(F32)
        table = tab_ref[...]
        first = (dens * mm(rows, table) + wide).astype(BF16)
        pops = (dens * mm(first, table) + wide).astype(BF16)
        return rays, pops

    @pl.loop(0, CHUNKS - 1)
    def _(c):
        rays, pops = chunk(c)
        hot = jnp.where(iota((RAYS, ROWS), 0) == rays, 1.0, 0.0).astype(BF16)
        acc[...] += mm(hot, pops)

    rays, pops = chunk(CHUNKS - 1)

    pieces = [((mz >> 1) + k) & (PIECES - 1) for k in (2, 1, 3, 0)]

    def pair_copy(n):
        return pltpu.make_async_remote_copy(
            src_ref=sbuf.at[n], dst_ref=crecv.at[n], send_sem=c_ssem.at[n], recv_sem=c_rsem.at[n],
            device_id=(me, mx * 2 + 1 - core), device_id_type=MESH,
        )

    def x_copy(n, i):
        return pltpu.make_async_remote_copy(
            src_ref=xsend.at[n, i - 1], dst_ref=xrecv.at[n, i - 1], send_sem=x_ssem.at[n, i - 1],
            recv_sem=x_rsem.at[n, i - 1],
            device_id=(me, ((mx + i) & (N_X - 1)) * 2 + core), device_id_type=MESH,
        )

    def share(piece, member_x, member_core):
        at = piece * PIECE + (member_x * 2 + member_core) * SHARE
        return pl.ds(pl.multiple_of(at, SHARE), SHARE)

    def sum_cells(n):
        piece = pieces[n]
        here = pl.ds(pl.multiple_of(piece * PIECE, PIECE), PIECE)
        hot = jnp.where(iota((PIECE, ROWS), 0) + piece * PIECE == rays, 1.0, 0.0).astype(BF16)
        acc[here, :] += mm(hot, pops)
        for x in range(N_X):
            sbuf[n, x] = acc[share(piece, x, 1 - core), :].astype(BF16)
        pair_copy(n).start()

    def sum_pair(n):
        pair_copy(n).wait_recv()
        for i in (2, 1, 3):
            x = (mx + i) & (N_X - 1)
            both = acc[share(pieces[n], x, core), :] + crecv[n, x].astype(F32)
            xsend[n, i - 1] = both.astype(BF16)
            x_copy(n, i).start()

    def sum_x(n):
        piece = pieces[n]
        total = acc[share(piece, mx, core), :] + crecv[n, mx].astype(F32)
        for i in (1, 3, 2):
            x_copy(n, i).wait_recv()
            total = total + xrecv[n, i - 1].astype(F32)
        total = total.astype(BF16)
        for j in range(PIECE_BINS):
            ysend[piece * PIECE_BINS + j] = total[2 * j : 2 * j + 2, :]

        @pl.loop(0, PIECE_BINS)
        def _(j):
            to = piece * PIECE_BINS + ((me + j) & (PIECE_BINS - 1))

            @pl.when(to != me)
            def _():
                pltpu.make_async_remote_copy(
                    src_ref=ysend.at[to], dst_ref=yrecv.at[me], send_sem=y_ssem, recv_sem=y_rsem,
                    device_id=(to, wave), device_id_type=MESH,
                ).start()

    sum_cells(0)
    sum_cells(1)
    sum_pair(0)
    sum_cells(2)
    sum_pair(1)
    sum_cells(3)
    sum_pair(2)
    sum_pair(3)
    for n in range(PIECES):
        sum_x(n)

    pltpu.make_async_copy(ysend.at[me], yrecv.at[me], y_rsem).start()
    pltpu.make_async_copy(yrecv, yrecv, y_rsem).wait()
    asend[...] = jnp.sum(yrecv[...].astype(F32), axis=0)
    for i in range(1, N_WAVE):
        pltpu.make_async_remote_copy(
            src_ref=asend, dst_ref=arecv.at[wave], send_sem=a_ssem, recv_sem=a_rsem,
            device_id=(me, (wave + i) & (N_WAVE - 1)), device_id_type=MESH,
        ).start()
    pltpu.make_async_copy(asend, arecv.at[wave], a_rsem).start()

    rest = pl.ds(0, N_BIN - 1)
    pltpu.make_async_copy(esend.at[rest], esend.at[rest], e_ssem).wait()
    pltpu.make_async_copy(send.at[rest], send.at[rest], s_sem).wait()
    for n in range(PIECES):
        pair_copy(n).wait_send()
        for i in (1, 2, 3):
            x_copy(n, i).wait_send()
    pltpu.make_async_copy(ysend.at[rest], ysend.at[rest], y_ssem).wait()

    pltpu.make_async_copy(arecv, arecv, a_rsem).wait()
    for w in range(N_WAVE):
        out_ref[2 * w : 2 * w + 2, :] = arecv[w]
    store = pltpu.make_async_copy(out_ref, out_any, load_sem.at[0])
    store.start()
    others = pl.ds(0, N_WAVE - 1)
    pltpu.make_async_copy(arecv.at[others], arecv.at[others], a_ssem).wait()
    store.wait()


def per_device(sources, density, temp_bins, ray_index, rate_tables, line_table):
    hbm = pl.BlockSpec(memory_space=pltpu.HBM)
    dma = pltpu.SemaphoreType.DMA
    whole_rays = pl.pallas_call(
        kernel,
        out_shape=jax.ShapeDtypeStruct((RAYS // N_BIN, LEVELS), F32),
        in_specs=[hbm] * 5,
        out_specs=pl.BlockSpec(memory_space=pl.ANY),
        scratch_shapes=[
            pltpu.VMEM((CELLS, LEVELS), BF16),
            pltpu.VMEM((CELLS // 128, 128), BF16),
            pltpu.VMEM((CELLS // 128, 128), jnp.int32),
            pltpu.VMEM((CELLS // 128, 128), jnp.int32),
            pltpu.VMEM((LEVELS, LEVELS), BF16),
            pltpu.VMEM((RAYS // N_BIN, LEVELS), F32),
            dma((5,)),
            pltpu.VMEM((N_BIN, CAP, LEVELS), BF16),
            pltpu.VMEM((N_BIN, 1, 128), F32),
            pltpu.VMEM((N_BIN, CAP, LEVELS), BF16),
            pltpu.VMEM((N_BIN, 1, 128), F32),
            pltpu.VMEM((RAYS, LEVELS), F32),
            pltpu.VMEM((PIECES, N_X, SHARE, LEVELS), BF16),
            pltpu.VMEM((PIECES, N_X, SHARE, LEVELS), BF16),
            pltpu.VMEM((PIECES, N_X - 1, SHARE, LEVELS), BF16),
            pltpu.VMEM((PIECES, N_X - 1, SHARE, LEVELS), BF16),
            pltpu.VMEM((N_BIN, 2, LEVELS), BF16),
            pltpu.VMEM((N_BIN, 2, LEVELS), BF16),
            pltpu.VMEM((2, LEVELS), F32),
            pltpu.VMEM((N_WAVE, 2, LEVELS), F32),
            dma, dma, dma((CHUNKS,)), dma((CHUNKS,)), dma((PIECES,)), dma((PIECES,)),
            dma((PIECES, N_X - 1)), dma((PIECES, N_X - 1)),
            dma, dma, dma, dma,
        ],
        compiler_params=pltpu.CompilerParams(
            collective_id=0, has_side_effects=True, vmem_limit_bytes=24 * 1024 * 1024
        ),
        name="populations",
    )(*(pltpu.with_memory_space_constraint(a, pltpu.HBM) for a in (
        sources,
        density.reshape(4, 128),
        temp_bins.reshape(4, 128),
        ray_index.reshape(4, 128),
        rate_tables,
    )))
    return jnp.dot(
        whole_rays,
        line_table.astype(F32),
        precision=lax.Precision.HIGHEST,
        preferred_element_type=F32,
    )


def solution(mesh):
    in_specs = (
        P(("bin", "wave"), None),
        P(("bin", "wave")),
        P(("bin", "wave"), None),
        P(("bin", "wave")),
        P("bin", None, None),
        P(None, "wave"),
    )
    return jax.shard_map(
        per_device, mesh=mesh, in_specs=in_specs, out_specs=P("bin", "wave"), check_vma=False
    )
```

time: 54.1 us -> 49.4 us (0.913)
  Pallas kernels: 52.2 us -> 48.3 us
  matrix products: 1.67 us -> 0.95 us
    pallas_call x1, Pallas kernels: 52.2 us -> 48.3 us  [per_device(): pl.pallas_call(kernel, out_shape=jax.ShapeDtypeStruct((RAYS // N_BIN, LEV...]
    dot_general x1, matrix products: 1.67 us -> 0.95 us  [per_device(): jnp.dot(whole_rays, line_table.astype(F32), precision=lax.Precision.HIGHE...]
where the time goes in v3:
time: 49.4 us; the launch traced here: 49.3 us
  Pallas kernels  48.3 us (98%)
  matrix products  0.95 us (2%)
    pallas_call x1, Pallas kernels, per_device(): pl.pallas_call(kernel, out_shape=jax.ShapeDtypeStruct((RAYS // N_BIN, LEV...  48.3 us

profile of v3, /device:TPU:1, one launch (start us, length us, event | category | flops | bytes accessed | tf_op | source)
XLA Modules:
  0.0 49.3 jit_solution(13869989865950580248)
XLA Ops:
  0.0 0.0 copy-start
  0.0 48.3 %populations.1 = f32[16,256]{1,0:T(8,128)S(1)} custom-call(bf16[512,256]{1,0:T(8,128)(2,1)} %src_hbm.1, bf16[4,128]{1,0:T(4,128)(2,1)} %bitcast.7, s32[4,128]{1,0:T(4,128)} %bitcast.5, s32[4,128]{1,0:T(4,128)} %bitcast.6, bf16[1,256,256]{2,1,0:T(8,128)(2,1)} %tab_hbm.1), custom_call_target="tpu_custom_call" | custom-call | tf_op jit(solution)/shard_map/populations/pallas_call | solution.py:270
  48.3 0.0 copy-done
  48.3 1.0 %fusion = f32[16,1024]{1,0:T(8,128)} fusion(f32[16,256]{1,0:T(8,128)S(1)} %populations.1, bf16[256,1024]{1,0:T(8,128)(2,1)S(1)} %copy-done), kind=kOutput, calls=%fused_computation | convolution fusion | flops 50331648 | bytes 606208 | tf_op jit(solution)/shard_map/dot_general | solution.py:311
Async XLA Ops:
  0.0 48.3 %copy-start = (bf16[256,1024]{1,0:T(8,128)(2,1)S(1)}, bf16[256,1024]{1,0:T(8,128)(2,1)}, u32[]{:S(2)}) copy-start(bf16[256,1024]{1,0:T(8,128)(2,1)} %param.11) | copy-start | bytes 1572868

commit v4 on v3

--- a/solution.py
+++ b/solution.py
@@ -25,26 +25,58 @@
 SHARE = PIECE // N_WAVE
 
 
+STEPS = ((1, 0), (0, -1), (-1, 0), (0, 1))
+
+
+def signed(d):
+    return (d + SIDE // 2 - 1) % SIDE - SIDE // 2 + 1
+
+
+def reach(offset):
+    return sum(abs(signed(d)) for d in offset)
+
+
 def turned(offset):
     return offset[1], (-offset[0]) % SIDE
 
 
-def reach(offset):
-    return sum(min(d, SIDE - d) for d in offset)
-
-
-def far_first():
-    order = []
+def before(offset, step):
+    return (offset[0] - step[0]) % SIDE, (offset[1] - step[1]) % SIDE
+
+
+def plan():
+    half = SIDE // 2
+    last = [(half, half), (0, half), (half, 0), (0, 0)]
+    groups, seen = [], set(last)
     offsets = [(dz, dy) for dz in range(SIDE) for dy in range(SIDE)]
     for offset in sorted(offsets, key=lambda o: (-reach(o), o)):
-        for _ in range(4):
-            if offset not in order:
-                order.append(offset)
+        if offset in seen:
+            continue
+        dz, dy = signed(offset[0]), signed(offset[1])
+        along = (1 if dz > 0 else -1, 0) if abs(dz) >= abs(dy) else (0, 1 if dy > 0 else -1)
+        group = [None] * 4
+        for n in range(4):
+            group[(STEPS.index(along) + n) % 4] = offset
+            seen.add(offset)
             offset = turned(offset)
-    return order
-
-
-ORDER = far_first()
+        groups.append(group)
+    return groups + [last]
+
+
+GROUPS = plan()
+PER_CHUNK = len(GROUPS) // CHUNKS
+SLOTS = []
+for c in range(CHUNKS):
+    for d, step in enumerate(STEPS):
+        for group in GROUPS[c * PER_CHUNK : (c + 1) * PER_CHUNK]:
+            owner = group[d]
+            SLOTS.append((owner, before(owner, step) if owner != (0, 0) else owner))
+
+
+SEND = sorted(
+    range(N_BIN), key=lambda k: (-reach(SLOTS[k][1]), k // PER, k % PER_CHUNK, k % PER // PER_CHUNK)
+)
+PLANE = [owner for owner, _ in SLOTS if owner != (0, 0)]
 
 
 def iota(shape, dim):
@@ -68,7 +100,7 @@
     src_hbm, den_hbm, bins_hbm, ray_hbm, tab_hbm, out_any,
     src_ref, den_ref, bins_ref, ray_ref, tab_ref, out_ref, load_sem,
     send, esend, recv, erecv, acc, sbuf, crecv, xsend, xrecv, ysend, yrecv, asend, arecv,
-    s_sem, e_ssem, r_sem, e_rsem, c_ssem, c_rsem, x_ssem, x_rsem, y_ssem, y_rsem, a_ssem, a_rsem,
+    near, t_ssem, t_rsem, met, s_sem, e_ssem, r_sem, e_rsem, c_ssem, c_rsem, x_ssem, x_rsem, y_ssem, y_rsem, a_ssem, a_rsem,
 ):
     me = lax.axis_index("bin")
     wave = lax.axis_index("wave")
@@ -88,12 +120,51 @@
     for load in loads:
         load.start()
     barrier = pltpu.get_barrier_semaphore()
-    for offset in ORDER[:-1]:
-        pl.semaphore_signal(barrier, inc=1, device_id=(peer(offset), wave), device_id_type=MESH)
-    for i in range(1, N_WAVE):
-        pl.semaphore_signal(
-            barrier, inc=1, device_id=(me, (wave + i) & (N_WAVE - 1)), device_id_type=MESH
+
+    def greet(bin_at, wave_at):
+        pl.semaphore_signal(barrier, inc=1, device_id=(bin_at, wave_at), device_id_type=MESH)
+
+    first_core = mx * 2
+    for offset in sorted(PLANE, key=lambda o: -reach(o)):
+        greet(peer(offset), first_core)
+    for i in range(1, N_X):
+        greet(me, ((mx + i) & (N_X - 1)) * 2)
+    for step in STEPS:
+        greet(peer(step), first_core + 1)
+    greet(me, first_core + 1 - core)
+
+    def table_copy(d):
+        back = (-STEPS[d][0], -STEPS[d][1])
+        return pltpu.make_async_remote_copy(
+            src_ref=tab_ref, dst_ref=near.at[d], send_sem=t_ssem.at[d], recv_sem=t_rsem.at[d],
+            device_id=(peer(back), wave), device_id_type=MESH,
         )
+
+    def ship():
+        for k in SEND:
+            owner, host = SLOTS[k]
+            own, to = peer(owner), peer(host)
+            for out, into, s, r in ((esend, erecv, e_ssem, e_rsem), (send, recv, s_sem, r_sem)):
+                if host == (0, 0):
+                    pltpu.make_async_copy(out.at[own], into.at[k], r.at[k // PER]).start()
+                else:
+                    pltpu.make_async_remote_copy(
+                        src_ref=out.at[own], dst_ref=into.at[k], send_sem=s,
+                        recv_sem=r.at[k // PER], device_id=(to, wave), device_id_type=MESH,
+                    ).start()
+
+    @pl.when(core == 1)
+    def _():
+        pl.semaphore_wait(barrier, 2 * len(STEPS) + 1)
+        pl.semaphore_signal(met.at[0], inc=1, device_id=(me, first_core), device_id_type=MESH)
+
+    @pl.when(core == 0)
+    def _():
+        pl.semaphore_wait(met.at[0], 1)
+
+    loads[4].wait()
+    for d in range(4):
+        table_copy(d).start()
 
     for load in loads[:3]:
         load.wait()
@@ -117,30 +188,43 @@
         esend[b] = extras[b : b + 1, :]
     loads[3].wait()
 
-    @pl.loop(0, CHUNKS)
-    def _(c):
+    def pack(c):
         hot = jnp.where(iota((ROWS, CELLS), 0) + c * ROWS == slot, 1.0, 0.0).astype(BF16)
         packed = mm(hot, src_ref[...]).astype(BF16)
         send[pl.ds(c * PER, PER)] = packed.reshape(PER, CAP, LEVELS)
 
-    pl.semaphore_wait(barrier, N_BIN + N_WAVE - 2)
-
-    for k, offset in enumerate(ORDER[:-1]):
-        to = peer(offset)
-        for out, into, s, r in ((esend, erecv, e_ssem, e_rsem), (send, recv, s_sem, r_sem)):
-            pltpu.make_async_remote_copy(
-                src_ref=out.at[to], dst_ref=into.at[k], send_sem=s, recv_sem=r.at[k // PER],
-                device_id=(to, wave), device_id_type=MESH,
-            ).start()
-    pltpu.make_async_copy(esend.at[me], erecv.at[N_BIN - 1], e_rsem.at[CHUNKS - 1]).start()
-    pltpu.make_async_copy(send.at[me], recv.at[N_BIN - 1], r_sem.at[CHUNKS - 1]).start()
-
+    @pl.loop(0, CHUNKS)
+    def _(c):
+        pack(c)
+
+    @pl.when(core == 0)
+    def _():
+        pl.semaphore_wait(barrier, 2 * (N_BIN - 1) + 2 * (N_X - 1) + 1)
+        pl.semaphore_signal(met.at[1], inc=1, device_id=(me, first_core + 1), device_id_type=MESH)
+
+    @pl.when(core == 1)
+    def _():
+        pl.semaphore_wait(met.at[1], 1)
+
+    ship()
     acc[...] = jnp.zeros_like(acc)
-    loads[4].wait()
+    for d in range(4):
+        table_copy(d).wait_recv()
     ones = jnp.ones((128, LEVELS), BF16)
     ones8 = jnp.ones((8, 128), BF16)
 
-    def chunk(c):
+    quarter = ROWS // 4
+
+    def by_table(rows, last):
+        parts = [mm(rows[d * quarter : (d + 1) * quarter], near[d]) for d in range(3)]
+        if last:
+            parts.append(mm(rows[3 * quarter : ROWS - CAP], near[3]))
+            parts.append(mm(rows[ROWS - CAP :], tab_ref[...]))
+        else:
+            parts.append(mm(rows[3 * quarter :], near[3]))
+        return jnp.concatenate(parts, axis=0)
+
+    def chunk(c, last=False):
         block = pl.ds(c * PER, PER)
         pltpu.make_async_copy(erecv.at[block], erecv.at[block], e_rsem.at[c]).wait()
         pltpu.make_async_copy(recv.at[block], recv.at[block], r_sem.at[c]).wait()
@@ -154,9 +238,8 @@
         rays = nt(ones8, coded.astype(BF16))[0:1, :].astype(jnp.int32)
         rows = recv[block].reshape(ROWS, LEVELS)
         wide = rows.astype(F32)
-        table = tab_ref[...]
-        first = (dens * mm(rows, table) + wide).astype(BF16)
-        pops = (dens * mm(first, table) + wide).astype(BF16)
+        first = (dens * by_table(rows, last) + wide).astype(BF16)
+        pops = (dens * by_table(first, last) + wide).astype(BF16)
         return rays, pops
 
     @pl.loop(0, CHUNKS - 1)
@@ -165,7 +248,7 @@
         hot = jnp.where(iota((RAYS, ROWS), 0) == rays, 1.0, 0.0).astype(BF16)
         acc[...] += mm(hot, pops)
 
-    rays, pops = chunk(CHUNKS - 1)
+    rays, pops = chunk(CHUNKS - 1, last=True)
 
     pieces = [((mz >> 1) + k) & (PIECES - 1) for k in (2, 1, 3, 0)]
 
@@ -245,9 +328,12 @@
         ).start()
     pltpu.make_async_copy(asend, arecv.at[wave], a_rsem).start()
 
+    for d in range(4):
+        table_copy(d).wait_send()
+    away = pl.ds(0, sum(host != (0, 0) for _, host in SLOTS))
+    pltpu.make_async_copy(esend.at[away], esend.at[away], e_ssem).wait()
+    pltpu.make_async_copy(send.at[away], send.at[away], s_sem).wait()
     rest = pl.ds(0, N_BIN - 1)
-    pltpu.make_async_copy(esend.at[rest], esend.at[rest], e_ssem).wait()
-    pltpu.make_async_copy(send.at[rest], send.at[rest], s_sem).wait()
     for n in range(PIECES):
         pair_copy(n).wait_send()
         for i in (1, 2, 3):
@@ -256,12 +342,9 @@
 
     pltpu.make_async_copy(arecv, arecv, a_rsem).wait()
     for w in range(N_WAVE):
-        out_ref[2 * w : 2 * w + 2, :] = arecv[w]
-    store = pltpu.make_async_copy(out_ref, out_any, load_sem.at[0])
-    store.start()
+        out_any[2 * w : 2 * w + 2, :] = arecv[w]
     others = pl.ds(0, N_WAVE - 1)
     pltpu.make_async_copy(arecv.at[others], arecv.at[others], a_ssem).wait()
-    store.wait()
 
 
 def per_device(sources, density, temp_bins, ray_index, rate_tables, line_table):
@@ -271,7 +354,7 @@
         kernel,
         out_shape=jax.ShapeDtypeStruct((RAYS // N_BIN, LEVELS), F32),
         in_specs=[hbm] * 5,
-        out_specs=pl.BlockSpec(memory_space=pl.ANY),
+        out_specs=pl.BlockSpec(memory_space=pltpu.VMEM),
         scratch_shapes=[
             pltpu.VMEM((CELLS, LEVELS), BF16),
             pltpu.VMEM((CELLS // 128, 128), BF16),
@@ -293,6 +376,8 @@
             pltpu.VMEM((N_BIN, 2, LEVELS), BF16),
             pltpu.VMEM((2, LEVELS), F32),
             pltpu.VMEM((N_WAVE, 2, LEVELS), F32),
+            pltpu.VMEM((4, LEVELS, LEVELS), BF16),
+            dma((4,)), dma((4,)), pltpu.SemaphoreType.REGULAR((2,)),
             dma, dma, dma((CHUNKS,)), dma((CHUNKS,)), dma((PIECES,)), dma((PIECES,)),
             dma((PIECES, N_X - 1)), dma((PIECES, N_X - 1)),
             dma, dma, dma, dma,

time: 49.4 us -> 47.8 us (0.968)
  Pallas kernels: 48.3 us -> 46.7 us
    pallas_call x1, Pallas kernels: 48.3 us -> 46.7 us  [per_device(): pl.pallas_call(kernel, out_shape=jax.ShapeDtypeStruct((RAYS // N_BIN, LEV...]
where the time goes in v4:
time: 47.8 us; the launch traced here: 47.7 us
  Pallas kernels  46.7 us (98%)
  matrix products  0.95 us (2%)
    pallas_call x1, Pallas kernels, per_device(): pl.pallas_call(kernel, out_shape=jax.ShapeDtypeStruct((RAYS // N_BIN, LEV...  46.7 us

profile of v4, /device:TPU:1, one launch (start us, length us, event | category | flops | bytes accessed | tf_op | source)
XLA Modules:
  0.0 47.7 jit_solution(18160124286578837079)
XLA Ops:
  0.0 0.0 copy-start
  0.0 46.7 %populations.1 = f32[16,256]{1,0:T(8,128)S(1)} custom-call(bf16[512,256]{1,0:T(8,128)(2,1)} %src_hbm.1, bf16[4,128]{1,0:T(4,128)(2,1)} %bitcast.7, s32[4,128]{1,0:T(4,128)} %bitcast.5, s32[4,128]{1,0:T(4,128)} %bitcast.6, bf16[1,256,256]{2,1,0:T(8,128)(2,1)} %tab_hbm.1), custom_call_target="tpu_custom_call" | custom-call | tf_op jit(solution)/shard_map/populations/pallas_call | solution.py:353
  46.7 0.0 copy-done
  46.7 1.0 %fusion = f32[16,1024]{1,0:T(8,128)} fusion(f32[16,256]{1,0:T(8,128)S(1)} %populations.1, bf16[256,1024]{1,0:T(8,128)(2,1)S(1)} %copy-done), kind=kOutput, calls=%fused_computation | convolution fusion | flops 50331648 | bytes 606208 | tf_op jit(solution)/shard_map/dot_general | solution.py:396
Async XLA Ops:
  0.0 46.7 %copy-start = (bf16[256,1024]{1,0:T(8,128)(2,1)S(1)}, bf16[256,1024]{1,0:T(8,128)(2,1)}, u32[]{:S(2)}) copy-start(bf16[256,1024]{1,0:T(8,128)(2,1)} %param.11) | copy-start | bytes 1572868

commit v5 on v4

--- a/solution.py
+++ b/solution.py
@@ -296,12 +296,11 @@
         for j in range(PIECE_BINS):
             ysend[piece * PIECE_BINS + j] = total[2 * j : 2 * j + 2, :]
 
-        @pl.loop(0, PIECE_BINS)
-        def _(j):
+        for j in sorted(range(PIECE_BINS), key=lambda j: -abs(signed(j % SIDE))):
             to = piece * PIECE_BINS + ((me + j) & (PIECE_BINS - 1))
 
             @pl.when(to != me)
-            def _():
+            def _(to=to):
                 pltpu.make_async_remote_copy(
                     src_ref=ysend.at[to], dst_ref=yrecv.at[me], send_sem=y_ssem, recv_sem=y_rsem,
                     device_id=(to, wave), device_id_type=MESH,
@@ -321,7 +320,7 @@
     pltpu.make_async_copy(ysend.at[me], yrecv.at[me], y_rsem).start()
     pltpu.make_async_copy(yrecv, yrecv, y_rsem).wait()
     asend[...] = jnp.sum(yrecv[...].astype(F32), axis=0)
-    for i in range(1, N_WAVE):
+    for i in (4, 5, 3, 2, 6, 7, 1):
         pltpu.make_async_remote_copy(
             src_ref=asend, dst_ref=arecv.at[wave], send_sem=a_ssem, recv_sem=a_rsem,
             device_id=(me, (wave + i) & (N_WAVE - 1)), device_id_type=MESH,

time: 47.8 us -> 47.7 us (level)
  no operation moved by 1% of the time
where the time goes in v5:
time: 47.7 us; the launch traced here: 47.6 us
  Pallas kernels  46.6 us (98%)
  matrix products  0.95 us (2%)
    pallas_call x1, Pallas kernels, per_device(): pl.pallas_call(kernel, out_shape=jax.ShapeDtypeStruct((RAYS // N_BIN, LEV...  46.6 us

profile of v5, /device:TPU:1, one launch (start us, length us, event | category | flops | bytes accessed | tf_op | source)
XLA Modules:
  0.0 47.6 jit_solution(11862787038357139174)
XLA Ops:
  0.0 0.0 copy-start
  0.0 46.6 %populations.1 = f32[16,256]{1,0:T(8,128)S(1)} custom-call(bf16[512,256]{1,0:T(8,128)(2,1)} %src_hbm.1, bf16[4,128]{1,0:T(4,128)(2,1)} %bitcast.7, s32[4,128]{1,0:T(4,128)} %bitcast.5, s32[4,128]{1,0:T(4,128)} %bitcast.6, bf16[1,256,256]{2,1,0:T(8,128)(2,1)} %tab_hbm.1), custom_call_target="tpu_custom_call" | custom-call | tf_op jit(solution)/shard_map/populations/pallas_call | solution.py:352
  46.6 0.0 copy-done
  46.6 1.0 %fusion = f32[16,1024]{1,0:T(8,128)} fusion(f32[16,256]{1,0:T(8,128)S(1)} %populations.1, bf16[256,1024]{1,0:T(8,128)(2,1)S(1)} %copy-done), kind=kOutput, calls=%fused_computation | convolution fusion | flops 50331648 | bytes 606208 | tf_op jit(solution)/shard_map/dot_general | solution.py:395
Async XLA Ops:
  0.0 46.6 %copy-start = (bf16[256,1024]{1,0:T(8,128)(2,1)S(1)}, bf16[256,1024]{1,0:T(8,128)(2,1)}, u32[]{:S(2)}) copy-start(bf16[256,1024]{1,0:T(8,128)(2,1)} %param.11) | copy-start | bytes 1572868
